TPU v7x, 32 devices: a whole 2x2x4 slice. The times are simulated.
32 devices in a mesh: dp: 4 (over z), row: 4 (over y, core), col: 2 (over x).
Axes of the slice: x: 2, y: 2, z: 4, core: 2. Of those that a mesh axis runs over, the one named last changes fastest.
Arguments:
- tokens: bfloat16 [8192, 2048], P(('dp', 'col'), 'row'), may hold values from -6 to 6
- seq_ids: int32 [8192], P('dp'), may hold values from 0 to 7, as said below
- block_ids: int32 [8192], P('dp'), may hold values from 0 to 5, as said below
- positions: int32 [8192], P('dp'), may hold values from 0 to 1535, as said below
- norm1_gain: float32 [2048], P('row'), may hold values from 0.5 to 1.5
- norm2_gain: float32 [2048], P('row'), may hold values from 0.5 to 1.5
- w_query: bfloat16 [2048, 2048], P('row', 'col'), may hold values from -0.1875 to 0.1875
- w_kv: bfloat16 [2048, 256], P('row'), may hold values from -0.1875 to 0.1875
- w_out: bfloat16 [2048, 2048], P('col', 'row'), may hold values from -2 to 2
- w_gate: bfloat16 [2048, 5632], P('row', 'col'), may hold values from -0.125 to 0.125
- w_up: bfloat16 [2048, 5632], P('row', 'col'), may hold values from -0.125 to 0.125
- w_down: bfloat16 [5632, 2048], P('col', 'row'), may hold values from -0.078125 to 0.078125
- grad_output: float32 [8192, 2048], P(('dp', 'col'), 'row'), may hold values from -6 to 6
Outputs:
- output: float32 [8192, 2048], P(('dp', 'col'), 'row')
- input_grad: float32 [8192, 2048], P(('dp', 'col'), 'row')
- grad_query: float32 [4, 512, 2048], P('row', 'dp', 'col')
- grad_kv: float32 [4, 512, 256], P('row', ('dp', 'col'))
- grad_out: float32 [2, 1024, 2048], P('col', 'dp', 'row')
- grad_gate: float32 [4, 512, 5632], P('row', 'dp', 'col')
- grad_up: float32 [4, 512, 5632], P('row', 'dp', 'col')
- grad_down: float32 [2, 2816, 2048], P('col', 'dp', 'row')
- grad_norm1: float32 [4, 512], P('row', ('dp', 'col'))
- grad_norm2: float32 [4, 512], P('row', ('dp', 'col'))
Inputs may be any that keep to these rules, and one draw needn't show every extreme that they name: `seq_ids`: tokens of one sequence lie in one aligned run of 2048 tokens; each run holds two sequences of whole 256-token blocks, each a quarter of the run or more; in the first run the first sequence has exactly 2 blocks. block_ids equal positions // 256. positions count from 0 at each sequence's first token.
All inputs are finite; a program needn't handle non-finite values.
Results may differ from a plain program's by a relative error of at most 0.023.
Values may be sent and summed in bfloat16 or wider, within the bound.
No kernel may reach another device: no remote copies, remote signals or barrier semaphores. Data moves between devices by JAX's collectives and lax.ppermute only.
A program may use at most 256 MiB of HBM per device.

v0:
```python
import jax
import jax.numpy as jnp
from jax import lax
from jax.sharding import PartitionSpec as P

D = 2048
EPS = 1e-05
ROPE_BASE = 500000.0
MASKED = -1e30
CONTRACT_ROWS = (((0,), (0,)), ((), ()))
CONTRACT_LAST = (((1,), (1,)), ((), ()))


def rope_tables(positions, head_width):
    halfway = head_width // 2
    frequency = ROPE_BASE ** (-2.0 * jnp.arange(halfway, dtype=jnp.float32) / head_width)
    angles = positions.astype(jnp.float32)[:, None] * frequency[None, :]
    return (jnp.cos(angles), jnp.sin(angles))


def rotate(operand, cosine, sine_part):
    halfway = operand.shape[-1] // 2
    first_half = operand[..., :halfway]
    second_half = operand[..., halfway:]
    return jnp.concatenate(
        [
            first_half * cosine - second_half * sine_part,
            second_half * cosine + first_half * sine_part,
        ],
        axis=-1,
    )


def rotate_back(operand, cosine, sine_part):
    halfway = operand.shape[-1] // 2
    first_half = operand[..., :halfway]
    second_half = operand[..., halfway:]
    return jnp.concatenate(
        [
            first_half * cosine + second_half * sine_part,
            second_half * cosine - first_half * sine_part,
        ],
        axis=-1,
    )


def row_total(operand):
    return lax.psum(operand, "row")


def gather_columns(operand):
    return lax.all_gather(operand, "col", axis=0, tiled=True)


def spread_columns(operand):
    return lax.psum_scatter(
        operand.astype(jnp.bfloat16), "col", scatter_dimension=0, tiled=True
    ).astype(jnp.float32)


def spread_rows(gathered, matrix, contract_dim):
    return lax.psum_scatter(
        lax.dot_general(
            gathered,
            matrix,
            (((1,), (contract_dim,)), ((), ())),
            preferred_element_type=jnp.float32,
        ),
        "row",
        scatter_dimension=0,
        tiled=True,
    )


def fold_rows(operand, matrix, contract_dim, partner, keeping):
    full_rows = operand.shape[0] * lax.axis_size("row")
    grad_shape = (partner.shape[1], operand.shape[1]) if partner is not None else (1, 1)
    grad_zero = jnp.zeros(grad_shape, jnp.float32)
    kept_zero = jnp.zeros((full_rows, operand.shape[1]) if keeping else (1, 1), operand.dtype)
    shard_rows = lax.all_gather(operand, "row", axis=0, tiled=True)
    grad_acc = grad_zero
    kept_rows = kept_zero
    row_block = lax.dot_general(
        shard_rows, matrix, (((1,), (contract_dim,)), ((), ())), preferred_element_type=jnp.float32
    )
    if partner is not None:
        grad_acc = lax.dot_general(
            partner, shard_rows, CONTRACT_ROWS, preferred_element_type=jnp.float32
        )
    if keeping:
        kept_rows = shard_rows
    return (row_block, grad_acc, kept_rows)


def norm_forward(residual, gain):
    rms_factor = lax.rsqrt(row_total(jnp.sum(residual * residual, axis=1)) / D + EPS)[:, None]
    return (rms_factor, (residual * rms_factor * gain[None, :]).astype(jnp.bfloat16))


def norm_backward(residual, rms_factor, gain, normed_grad):
    weighted = normed_grad * gain[None, :]
    inner_sum = row_total(jnp.sum(weighted * residual, axis=1))[:, None]
    input_part = (
        rms_factor * weighted - residual * (rms_factor * rms_factor * rms_factor) * inner_sum / D
    )
    return (input_part, jnp.sum(normed_grad * residual * rms_factor, axis=0))


def per_device(
    tokens,
    seq_ids,
    block_ids,
    positions,
    norm1_gain,
    norm2_gain,
    w_query,
    w_kv,
    w_out,
    w_gate,
    w_up,
    w_down,
    grad_output,
):
    row_count = lax.axis_size("row")
    full_rows = seq_ids.shape[0]
    slab_rows = full_rows // row_count
    slab_start = lax.axis_index("row") * slab_rows
    half_rows = tokens.shape[0]
    half_start = lax.axis_index("col") * half_rows
    head_width = w_kv.shape[1] // 2
    heads_local = w_query.shape[1] // head_width
    ff_local = w_gate.shape[1]
    score_scale = head_width ** (-0.5)
    w_both = jnp.concatenate([w_gate, w_up], axis=1)
    residual = tokens.astype(jnp.float32)
    factor_one, normed = norm_forward(residual, norm1_gain)
    gathered_in = gather_columns(normed)
    query_pre = spread_rows(gathered_in, w_query, 0)
    kv_pre = lax.psum(jnp.dot(gathered_in, w_kv, preferred_element_type=jnp.float32), "row")
    cosine_all, sine_all = rope_tables(positions, head_width)
    cosine_slab = lax.dynamic_slice_in_dim(cosine_all, slab_start, slab_rows, 0)[:, None, :]
    sine_slab = lax.dynamic_slice_in_dim(sine_all, slab_start, slab_rows, 0)[:, None, :]
    queries = rotate(
        query_pre.reshape(slab_rows, heads_local, head_width), cosine_slab, sine_slab
    ).astype(jnp.bfloat16)
    key_rows = rotate(kv_pre[:, :head_width], cosine_all, sine_all).astype(jnp.bfloat16)
    values = kv_pre[:, head_width:].astype(jnp.bfloat16)
    seq_slab = lax.dynamic_slice_in_dim(seq_ids, slab_start, slab_rows, 0)
    block_slab = lax.dynamic_slice_in_dim(block_ids, slab_start, slab_rows, 0)
    allowed = (seq_slab[:, None] == seq_ids[None, :]) & (block_ids[None, :] <= block_slab[:, None])
    head_queries = queries.transpose(1, 0, 2)

    def head_scores(query_head):
        scores = (
            lax.dot_general(query_head, key_rows, CONTRACT_LAST, preferred_element_type=jnp.float32)
            * score_scale
        )
        return jnp.where(allowed, scores, MASKED)

    def head_forward(query_head):
        scores = head_scores(query_head)
        row_max = jnp.max(scores, axis=1, keepdims=True)
        weights_exp = jnp.exp(scores - row_max)
        denominator = jnp.sum(weights_exp, axis=1, keepdims=True)
        probability = (weights_exp / denominator).astype(jnp.bfloat16)
        head_out = jnp.dot(probability, values, preferred_element_type=jnp.float32)
        return (head_out, (row_max + jnp.log(denominator))[:, 0])

    head_outs, log_totals = lax.map(head_forward, head_queries)
    attended = (
        head_outs.transpose(1, 0, 2)
        .reshape(slab_rows, heads_local * head_width)
        .astype(jnp.bfloat16)
    )
    out_product, _, kept_attended = fold_rows(attended, w_out, 0, None, True)
    hidden = residual + spread_columns(out_product)
    factor_two, normed_two = norm_forward(hidden, norm2_gain)
    gathered_mid = gather_columns(normed_two)
    both_proj = spread_rows(gathered_mid, w_both, 0)
    gate_proj = both_proj[:, :ff_local]
    up_proj = both_proj[:, ff_local:]
    sigmoid_gate = jax.nn.sigmoid(gate_proj)
    silu_gate = gate_proj * sigmoid_gate
    mixed_act = (silu_gate * up_proj).astype(jnp.bfloat16)
    down_product, _, kept_mixed = fold_rows(mixed_act, w_down, 0, None, True)
    output = hidden + spread_columns(down_product)
    down_grad = grad_output.astype(jnp.bfloat16)
    gathered_down = gather_columns(down_grad)
    mixed_grad = spread_rows(gathered_down, w_down, 1)
    grad_down_local = lax.dot_general(
        kept_mixed, gathered_down, CONTRACT_ROWS, preferred_element_type=jnp.float32
    )
    gate_grad = (
        mixed_grad * up_proj * sigmoid_gate * (1.0 + gate_proj * (1.0 - sigmoid_gate))
    ).astype(jnp.bfloat16)
    up_grad = (mixed_grad * silu_gate).astype(jnp.bfloat16)
    both_grad = jnp.concatenate([gate_grad, up_grad], axis=1)
    mid_product, grad_both_local, _ = fold_rows(both_grad, w_both, 1, gathered_mid, False)
    norm_two_part, gain_two_part = norm_backward(
        hidden, factor_two, norm2_gain, spread_columns(mid_product)
    )
    hidden_grad = grad_output + norm_two_part
    branch_grad = hidden_grad.astype(jnp.bfloat16)
    gathered_branch = gather_columns(branch_grad)
    attended_grad = spread_rows(gathered_branch, w_out, 1).astype(jnp.bfloat16)
    grad_out_local = lax.dot_general(
        kept_attended, gathered_branch, CONTRACT_ROWS, preferred_element_type=jnp.float32
    )
    head_grads = attended_grad.reshape(slab_rows, heads_local, head_width).transpose(1, 0, 2)

    def head_backward(running, head_inputs):
        key_acc, value_acc = running
        query_head, grad_head, log_total = head_inputs
        probs_full = jnp.exp(head_scores(query_head) - log_total[:, None])
        probs_low = probs_full.astype(jnp.bfloat16)
        value_acc = value_acc + lax.dot_general(
            probs_low, grad_head, CONTRACT_ROWS, preferred_element_type=jnp.float32
        )
        prob_grad = lax.dot_general(
            grad_head, values, CONTRACT_LAST, preferred_element_type=jnp.float32
        )
        row_dot = jnp.sum(probs_full * prob_grad, axis=1, keepdims=True)
        score_grad = (probs_full * (prob_grad - row_dot)).astype(jnp.bfloat16)
        query_grad = jnp.dot(score_grad, key_rows, preferred_element_type=jnp.float32) * score_scale
        key_acc = (
            key_acc
            + lax.dot_general(
                score_grad, query_head, CONTRACT_ROWS, preferred_element_type=jnp.float32
            )
            * score_scale
        )
        return ((key_acc, value_acc), query_grad)

    zero_rows = jnp.zeros((full_rows, head_width), jnp.float32)
    (key_acc, value_acc), query_grads = lax.scan(
        head_backward, (zero_rows, zero_rows), (head_queries, head_grads, log_totals)
    )
    key_total, value_total = (
        lax.psum(key_acc.astype(jnp.bfloat16), ("row", "col")).astype(jnp.float32),
        lax.psum(value_acc.astype(jnp.bfloat16), ("row", "col")).astype(jnp.float32),
    )
    query_pre_grad = (
        rotate_back(query_grads.transpose(1, 0, 2), cosine_slab, sine_slab)
        .reshape(slab_rows, heads_local * head_width)
        .astype(jnp.bfloat16)
    )
    kv_pre_grad = jnp.concatenate(
        [rotate_back(key_total, cosine_all, sine_all), value_total], axis=1
    ).astype(jnp.bfloat16)
    in_product, grad_query_local, _ = fold_rows(query_pre_grad, w_query, 1, gathered_in, False)
    kv_rows = lax.dynamic_slice_in_dim(kv_pre_grad, half_start, half_rows, 0)
    normed_grad = spread_columns(in_product) + lax.dot_general(
        kv_rows, w_kv, CONTRACT_LAST, preferred_element_type=jnp.float32
    )
    grad_kv_local = lax.dot_general(
        normed, kv_rows, CONTRACT_ROWS, preferred_element_type=jnp.float32
    )
    norm_one_part, gain_one_part = norm_backward(residual, factor_one, norm1_gain, normed_grad)
    input_grad = hidden_grad + norm_one_part
    reduced = (
        lax.psum_scatter(
            grad_query_local.astype(jnp.bfloat16), "dp", scatter_dimension=0, tiled=True
        ).astype(jnp.float32),
        lax.psum_scatter(
            grad_out_local.astype(jnp.bfloat16), "dp", scatter_dimension=0, tiled=True
        ).astype(jnp.float32),
        lax.psum_scatter(
            grad_both_local[:, :ff_local].astype(jnp.bfloat16),
            "dp",
            scatter_dimension=0,
            tiled=True,
        ).astype(jnp.float32),
        lax.psum_scatter(
            grad_both_local[:, ff_local:].astype(jnp.bfloat16),
            "dp",
            scatter_dimension=0,
            tiled=True,
        ).astype(jnp.float32),
        lax.psum_scatter(
            grad_down_local.astype(jnp.bfloat16), "dp", scatter_dimension=0, tiled=True
        ).astype(jnp.float32),
    )
    small_sums = (
        lax.psum_scatter(
            grad_kv_local.astype(jnp.bfloat16), ("dp", "col"), scatter_dimension=0, tiled=True
        ).astype(jnp.float32),
        lax.psum_scatter(
            jnp.stack([gain_one_part, gain_two_part], axis=1).astype(jnp.bfloat16),
            ("dp", "col"),
            scatter_dimension=0,
            tiled=True,
        ).astype(jnp.float32),
    )
    return (
        output,
        input_grad,
        reduced[0][None],
        small_sums[0][None],
        reduced[1][None],
        reduced[2][None],
        reduced[3][None],
        reduced[4][None],
        small_sums[1][:, 0][None, :],
        small_sums[1][:, 1][None, :],
    )


def solution(mesh):
    placed = (
        P(("dp", "col"), "row"),
        P("dp"),
        P("dp"),
        P("dp"),
        P("row"),
        P("row"),
        P("row", "col"),
        P("row", None),
        P("col", "row"),
        P("row", "col"),
        P("row", "col"),
        P("col", "row"),
        P(("dp", "col"), "row"),
    )
    return jax.shard_map(
        per_device,
        mesh=mesh,
        in_specs=placed,
        out_specs=(
            P(("dp", "col"), "row"),
            P(("dp", "col"), "row"),
            P("row", "dp", "col"),
            P("row", ("dp", "col"), None),
            P("col", "dp", "row"),
            P("row", "dp", "col"),
            P("row", "dp", "col"),
            P("col", "dp", "row"),
            P("row", ("dp", "col")),
            P("row", ("dp", "col")),
        ),
        check_vma=False,
    )
```

profile of v0, /device:TPU:0, one launch (start us, length us, event | category | flops | bytes accessed | tf_op | source)
XLA Modules:
  0.0 1890.7 jit_solution(8827306254039716388)
XLA Ops:
  8.9 8.4 psum.49
  21.1 33.5 %all-gather.9.cloned.1.call-done = bf16[2048,512]{1,0:T(8,128)(2,1)} async-done(((bf16[1024,512]{1,0:T(8,128)(2,1)}), bf16[2048,512]{1,0:T(8,128)(2,1)}) %all-gather.9.cloned.1.call-update) | async-done | bytes 2097168 | tf_op jit(solution)/shard_map/all_gather | solution.py:52
  58.3 7.5 fusion.66
  70.2 39.6 %all-reduce.4.cloned.1.call-done = f32[2048,256]{1,0:T(8,128)} async-done(((f32[2048,256]{1,0:T(8,128)}), f32[2048,256]{1,0:T(8,128)}) %all-reduce.4.cloned.1.call-update) | async-done | bytes 2097168 | tf_op jit(solution)/shard_map/psum | solution.py:139
  109.8 7.8 fusion.54
  122.4 62.0 %reduce-scatter.18.cloned.1.call-done = f32[512,1024]{1,0:T(8,128)} async-done(((f32[2048,1024]{1,0:T(8,128)}), f32[512,1024]{1,0:T(8,128)}) %reduce-scatter.18.cloned.1.call-update) | async-done | bytes 2097168 | tf_op jit(solution)/shard_map/reduce_scatter | solution.py:62
  192.5 66.3 %while.30 = (s32[]{:T(128)}, bf16[8,512,128]{1,2,0:T(8,128)(2,1)}, f32[8,512]{1,0:T(8,128)S(1)}, bf16[8,512,128]{2,1,0:T(8,128)(2,1)}, bf16[2048,128]{1,0:T(8,12...) while((s32[]{:T(128)}, bf16[8,512,128]{1,2,0:T(8,128)(2,1)}, ...), condition=%wide.region_7.8_spmd.clone.clone, body=%wide.region_4.7_spmd.clone.sunk.clone | while | flops 548404736 | bytes 30844036 | solution.py:169
  213.5 3.9 fusion.146
  258.9 34.6 %all-gather.11.cloned.1.call-done = bf16[2048,1024]{0,1:T(8,128)(2,1)} async-done(((bf16[512,1024]{0,1:T(8,128)(2,1)}), bf16[2048,1024]{0,1:T(8,128)(2,1)}) %all-gather.11.cloned.1.call-update) | async-done | bytes 4194320 | tf_op jit(solution)/shard_map/all_gather | solution.py:80
  293.5 6.2 convolution_convert_fusion.4
  302.7 29.0 %reduce-scatter.20.cloned.1.call-done = bf16[1024,512]{1,0:T(8,128)(2,1)} async-done(((bf16[2048,512]{1,0:T(8,128)(2,1)}), bf16[1024,512]{1,0:T(8,128)(2,1)}) %reduce-scatter.20.cloned.1.call-update) | async-done | bytes 1048592 | tf_op jit(solution)/shard_map/reduce_scatter | solution.py:56
  333.6 6.9 psum.51
  343.7 23.2 %all-gather.17.cloned.1.call-done = bf16[2048,512]{1,0:T(8,128)(2,1)} async-done(((bf16[1024,512]{1,0:T(8,128)(2,1)}), bf16[2048,512]{1,0:T(8,128)(2,1)}) %all-gather.17.cloned.1.call-update) | async-done | bytes 2097168 | tf_op jit(solution)/shard_map/all_gather | solution.py:52
  366.9 13.4 fusion.69
  386.0 16.3 all-gather.13.cloned.1.call-done
  402.2 34.2 %fusion.68 = f32[2048,5632]{1,0:T(8,128)} fusion(bf16[2048,512]{1,0:T(8,128)(2,1)} %all-gather.13.cloned.1.call-done, bf16[512,5632]{1,0:T(8,128)(2,1)} %constant_dynamic-update-slice_fusion.1), kind=kOutput, calls=%fused_computation.138 | convolution fusion | flops 11811160064 | bytes 54001664 | tf_op jit(solution)/shard_map/dot_general | solution.py:63
  436.6 135.3 %reduce-scatter.26.cloned.1.call-done = f32[512,2816]{1,0:T(8,128)} async-done(((f32[2048,2816]{1,0:T(8,128)}), f32[512,2816]{1,0:T(8,128)}) %reduce-scatter.26.cloned.1.call-update) | async-done | bytes 5767184 | tf_op jit(solution)/shard_map/reduce_scatter | solution.py:62
  571.8 318.6 %reduce-scatter.22.cloned.1.call-done = f32[512,5632]{1,0:T(8,128)} async-done(((f32[2048,5632]{1,0:T(8,128)}), f32[512,5632]{1,0:T(8,128)}) %reduce-scatter.22.cloned.1.call-update) | async-done | bytes 11534352 | tf_op jit(solution)/shard_map/reduce_scatter | solution.py:62
  890.4 8.8 multiply_convert_fusion.2
  902.3 143.1 %all-gather.19.cloned.1.call-done = bf16[2048,5632]{1,0:T(8,128)(2,1)} async-done(((bf16[512,5632]{1,0:T(8,128)(2,1)}), bf16[2048,5632]{1,0:T(8,128)(2,1)}) %all-gather.19.cloned.1.call-update) | async-done | bytes 23068688 | tf_op jit(solution)/shard_map/all_gather | solution.py:80
  1045.5 19.2 %convolution_convert_fusion.2 = bf16[2048,512]{1,0:T(8,128)(2,1)} fusion(bf16[2048,5632]{1,0:T(8,128)(2,1)} %all-gather.19.cloned.1.call-done, bf16[512,5632]{1,0:T(8,128)(2,1)} %constant_dynamic-update-slice_fusion.1), kind=kOutput, calls=%fused_computation.51 | convolution fusion | flops 11812208640 | bytes 30932992 | tf_op jit(solution)/shard_map/dot_general | solution.py:83
  1064.7 31.9 %reduce-scatter.28.cloned.1.call-done = bf16[1024,512]{1,0:T(8,128)(2,1)} async-done(((bf16[2048,512]{1,0:T(8,128)(2,1)}), bf16[1024,512]{1,0:T(8,128)(2,1)}) %reduce-scatter.28.cloned.1.call-update) | async-done | bytes 1048592 | tf_op jit(solution)/shard_map/reduce_scatter | solution.py:56
  1099.4 6.9 psum.52
  1110.1 32.3 %all-gather.21.cloned.1.call-done = bf16[2048,512]{1,0:T(8,128)(2,1)} async-done(((bf16[1024,512]{1,0:T(8,128)(2,1)}), bf16[2048,512]{1,0:T(8,128)(2,1)}) %all-gather.21.cloned.1.call-update) | async-done | bytes 2097168 | tf_op jit(solution)/shard_map/all_gather | solution.py:52
  1142.4 7.5 fusion.70
  1150.6 71.2 %reduce-scatter.30.cloned.1.call-done = f32[512,1024]{1,0:T(8,128)} async-done(((f32[2048,1024]{1,0:T(8,128)}), f32[512,1024]{1,0:T(8,128)}) %reduce-scatter.30.cloned.1.call-update) | async-done | bytes 2097168 | tf_op jit(solution)/shard_map/reduce_scatter | solution.py:62
  1224.6 133.2 %while.31 = (s32[]{:T(128)}, f32[2048,128]{1,0:T(8,128)}, f32[2048,128]{1,0:T(8,128)}, f32[8,512,128]{1,2,0:T(8,128)}, bf16[8,512,128]{2,1,0:T(8,128)(2,1)}, /*i...) while((s32[]{:T(128)}, f32[2048,128]{1,0:T(8,128)}, ...), condition=%wide.region_20.21_spmd.clone.clone, body=%wide.region_18.20_spmd.clone.sunk.clone | while | flops 1356135936 | bytes 87327544 | solution.py:235
  1234.4 4.0 fusion.157
  1364.3 11.0 convolution_convert_fusion.1
  1375.4 17.4 convolution_convert_fusion
  1396.6 6.2 convolution_convert_fusion.6
  1403.0 14.6 all-reduce.6.cloned.1.call-done
  1418.8 4.8 fusion.60
  1425.3 28.0 %all-gather.23.cloned.1.call-done = bf16[2048,1024]{0,1:T(8,128)(2,1)} async-done(((bf16[512,1024]{0,1:T(8,128)(2,1)}), bf16[2048,1024]{0,1:T(8,128)(2,1)}) %all-gather.23.cloned.1.call-update) | async-done | bytes 4194320 | tf_op jit(solution)/shard_map/all_gather | solution.py:80
  1453.3 6.2 convolution_convert_fusion.7
  1459.5 6.7 convolution_convert_fusion.3
  1466.3 9.9 convolution_convert_fusion.5
  1476.2 35.5 %reduce-scatter.44.cloned.1.call-done = bf16[704,512]{1,0:T(8,128)(2,1)} async-done(((bf16[2816,512]{1,0:T(8,128)(2,1)}), bf16[704,512]{1,0:T(8,128)(2,1)}) %reduce-scatter.44.cloned.1.call-update) | async-done | bytes 720912 | tf_op jit(solution)/shard_map/reduce_scatter | solution.py:279
  1514.2 55.9 %reduce-scatter.42.cloned.1.call-done = bf16[128,2816]{1,0:T(8,128)(2,1)} async-done(((bf16[512,2816]{1,0:T(8,128)(2,1)}), bf16[128,2816]{1,0:T(8,128)(2,1)}) %reduce-scatter.42.cloned.1.call-update) | async-done | bytes 720912 | tf_op jit(solution)/shard_map/reduce_scatter | solution.py:273
  1572.4 56.2 %reduce-scatter.40.cloned.1.call-done = bf16[128,2816]{1,0:T(8,128)(2,1)} async-done(((bf16[512,2816]{1,0:T(8,128)(2,1)}), bf16[128,2816]{1,0:T(8,128)(2,1)}) %reduce-scatter.40.cloned.1.call-update) | async-done | bytes 720912 | tf_op jit(solution)/shard_map/reduce_scatter | solution.py:267
  1630.8 27.0 %reduce-scatter.38.cloned.1.call-done = bf16[256,512]{1,0:T(8,128)(2,1)} async-done(((bf16[1024,512]{1,0:T(8,128)(2,1)}), bf16[256,512]{1,0:T(8,128)(2,1)}) %reduce-scatter.38.cloned.1.call-update) | async-done | bytes 262160 | tf_op jit(solution)/shard_map/reduce_scatter | solution.py:264
  1659.6 62.0 %reduce-scatter.36.cloned.1.call-done = bf16[64,256]{1,0:T(8,128)(2,1)} async-done(((bf16[512,256]{1,0:T(8,128)(2,1)}), bf16[64,256]{1,0:T(8,128)(2,1)}) %reduce-scatter.36.cloned.1.call-update) | async-done | bytes 32784 | tf_op jit(solution)/shard_map/reduce_scatter | solution.py:284
  1723.0 27.1 %reduce-scatter.34.cloned.1.call-done = bf16[128,1024]{1,0:T(8,128)(2,1)} async-done(((bf16[512,1024]{1,0:T(8,128)(2,1)}), bf16[128,1024]{1,0:T(8,128)(2,1)}) %reduce-scatter.34.cloned.1.call-update) | async-done | bytes 262160 | tf_op jit(solution)/shard_map/reduce_scatter | solution.py:261
  1751.9 31.6 %reduce-scatter.32.cloned.1.call-done = bf16[1024,512]{1,0:T(8,128)(2,1)} async-done(((bf16[2048,512]{1,0:T(8,128)(2,1)}), bf16[1024,512]{1,0:T(8,128)(2,1)}) %reduce-scatter.32.cloned.1.call-update) | async-done | bytes 1048592 | tf_op jit(solution)/shard_map/reduce_scatter | solution.py:56
  1788.1 6.8 psum.55
  1795.0 23.1 %reduce-scatter.24.cloned.1.call-done = bf16[1024,512]{1,0:T(8,128)(2,1)} async-done(((bf16[2048,512]{1,0:T(8,128)(2,1)}), bf16[1024,512]{1,0:T(8,128)(2,1)}) %reduce-scatter.24.cloned.1.call-update) | async-done | bytes 1048592 | tf_op jit(solution)/shard_map/reduce_scatter | solution.py:56
  1818.0 5.4 fusion.41
  1823.5 59.1 %reduce-scatter.46.cloned.1.call-done = bf16[64,2]{1,0:T(8,128)(2,1)} async-done(((bf16[512,2]{1,0:T(8,128)(2,1)}), bf16[64,2]{1,0:T(8,128)(2,1)}) %reduce-scatter.46.cloned.1.call-update) | async-done | bytes 272
  (373 shorter events, 275.6 us)
Async XLA Ops:
  7.2 359.7 %copy-start = (bf16[2816,512]{1,0:T(8,128)(2,1)S(1)}, bf16[2816,512]{1,0:T(8,128)(2,1)}, u32[]{:S(2)}) copy-start(bf16[2816,512]{1,0:T(8,128)(2,1)} %param.28) | copy-start | bytes 8650756
  7.2 47.4 %copy-start.15 = (bf16[512,256]{1,0:T(8,128)(2,1)S(1)}, bf16[512,256]{1,0:T(8,128)(2,1)}, u32[]{:S(2)}) copy-start(bf16[512,256]{1,0:T(8,128)(2,1)} %param.24) | copy-start | bytes 786436
  7.2 47.4 %all-gather.9.cloned.1.call-start = ((), (), s32[]{:S(2)}) async-start(), calls=%async_computation.15 | async-start | bytes 3145728 | tf_op jit(solution)/shard_map/all_gather | solution.py:52
  21.0 88.8 %all-reduce.4.cloned.1.call-start = ((), (), s32[]{:S(2)}) async-start(), calls=%async_computation.17 | async-start | bytes 4194304 | tf_op jit(solution)/shard_map/psum | solution.py:139
  58.2 126.1 %reduce-scatter.18.cloned.1.call-start = ((), (), s32[]{:S(2)}) async-start(), calls=%async_computation.16 | async-start | bytes 10485760 | tf_op jit(solution)/shard_map/reduce_scatter | solution.py:62
  65.8 227.7 %all-gather.11.cloned.1.call-start = ((), (), s32[]{:S(2)}) async-start(), calls=%async_computation.18 | async-start | bytes 5242880 | tf_op jit(solution)/shard_map/all_gather | solution.py:80
  66.5 51.1 %copy-start.16 = (f32[2048]{0:T(1024)}, f32[2048]{0:T(1024)S(1)}, u32[]{:S(2)}) copy-start(f32[2048]{0:T(1024)S(1)} %convert_element_type.116) | copy-start | bytes 24580
  69.1 48.4 %copy-start.26 = (f32[64]{0:T(128)}, f32[64]{0:T(128)S(1)}, u32[]{:S(2)}) copy-start(f32[64]{0:T(128)S(1)} %multiply_power_fusion) | copy-start | bytes 772
  117.7 69.5 %copy-start.11 = (f32[512,64]{0,1:T(8,128)}, f32[512,64]{0,1:T(8,128)S(1)}, u32[]{:S(2)}) copy-start(f32[512,64]{0,1:T(8,128)S(1)} %copy.36) | copy-start | bytes 393220
  258.8 72.8 %reduce-scatter.20.cloned.1.call-start = ((), (), s32[]{:S(2)}) async-start(), calls=%async_computation.19 | async-start | bytes 3145728 | tf_op jit(solution)/shard_map/reduce_scatter | solution.py:56
  299.7 67.2 %all-gather.17.cloned.1.call-start = ((), (), s32[]{:S(2)}) async-start(), calls=%async_computation.24 | async-start | bytes 3145728 | tf_op jit(solution)/shard_map/all_gather | solution.py:52
  302.4 38.1 %copy-start.20 = (f32[512]{0:T(512)S(1)}, f32[512]{0:T(512)}, u32[]{:S(2)}) copy-start(f32[512]{0:T(512)} %param.22) | copy-start | bytes 6148
  302.5 99.8 %all-gather.13.cloned.1.call-start = ((), (), s32[]{:S(2)}) async-start(), calls=%async_computation.20 | async-start | bytes 3145728 | tf_op jit(solution)/shard_map/all_gather | solution.py:52
  343.6 228.2 %reduce-scatter.26.cloned.1.call-start = ((), (), s32[]{:S(2)}) async-start(), calls=%async_computation.25 | async-start | bytes 28835840 | tf_op jit(solution)/shard_map/reduce_scatter | solution.py:62
  380.3 510.1 %reduce-scatter.22.cloned.1.call-start = ((), (), s32[]{:S(2)}) async-start(), calls=%async_computation.21 | async-start | bytes 57671680 | tf_op jit(solution)/shard_map/reduce_scatter | solution.py:62
  380.4 3.8 copy-start.10
  436.5 608.9 %all-gather.19.cloned.1.call-start = ((), (), s32[]{:S(2)}) async-start(), calls=%async_computation.26 | async-start | bytes 28835840 | tf_op jit(solution)/shard_map/all_gather | solution.py:80
  902.1 194.5 %reduce-scatter.28.cloned.1.call-start = ((), (), s32[]{:S(2)}) async-start(), calls=%async_computation.27 | async-start | bytes 3145728 | tf_op jit(solution)/shard_map/reduce_scatter | solution.py:56
  1064.6 77.8 %all-gather.21.cloned.1.call-start = ((), (), s32[]{:S(2)}) async-start(), calls=%async_computation.28 | async-start | bytes 3145728 | tf_op jit(solution)/shard_map/all_gather | solution.py:52
  1110.1 111.8 %reduce-scatter.30.cloned.1.call-start = ((), (), s32[]{:S(2)}) async-start(), calls=%async_computation.29 | async-start | bytes 10485760 | tf_op jit(solution)/shard_map/reduce_scatter | solution.py:62
  1150.0 214.3 %all-gather.15.cloned.1.call-start = ((), (), s32[]{:S(2)}) async-start(), calls=%async_computation.22 | async-start | bytes 14417920 | tf_op jit(solution)/shard_map/all_gather | solution.py:80
  1150.6 267.1 %all-reduce.6.cloned.1.call-start = ((), (), s32[]{:S(2)}) async-start(), calls=%async_computation.39 | async-start | bytes 2097152 | tf_op jit(solution)/shard_map/psum | solution.py:239
  1234.4 4.7 copy-start.3
  1251.5 3.9 copy-start.3
  1268.2 3.8 copy-start.3
  1284.7 3.8 copy-start.3
  1301.3 3.8 copy-start.3
  1317.8 3.8 copy-start.3
  1334.4 3.8 copy-start.3
  1350.9 3.8 copy-start.3
  1357.8 3.5 copy-start.13
  1360.8 92.4 %all-gather.23.cloned.1.call-start = ((), (), s32[]{:S(2)}) async-start(), calls=%async_computation.30 | async-start | bytes 5242880 | tf_op jit(solution)/shard_map/all_gather | solution.py:80
  1364.3 147.5 %reduce-scatter.44.cloned.1.call-start = ((), (), s32[]{:S(2)}) async-start(), calls=%async_computation.37 | async-start | bytes 3604480 | tf_op jit(solution)/shard_map/reduce_scatter | solution.py:279
  1375.4 194.7 %reduce-scatter.42.cloned.1.call-start = ((), (), s32[]{:S(2)}) async-start(), calls=%async_computation.36 | async-start | bytes 3604480 | tf_op jit(solution)/shard_map/reduce_scatter | solution.py:273
  1395.8 232.8 %reduce-scatter.40.cloned.1.call-start = ((), (), s32[]{:S(2)}) async-start(), calls=%async_computation.35 | async-start | bytes 3604480 | tf_op jit(solution)/shard_map/reduce_scatter | solution.py:267
  1396.5 261.3 %reduce-scatter.38.cloned.1.call-start = ((), (), s32[]{:S(2)}) async-start(), calls=%async_computation.34 | async-start | bytes 1310720 | tf_op jit(solution)/shard_map/reduce_scatter | solution.py:264
  1402.8 16.1 copy-start.17
  1402.8 16.1 copy-start.27
  1402.8 318.8 %reduce-scatter.36.cloned.1.call-start = ((), (), s32[]{:S(2)}) async-start(), calls=%async_computation.33 | async-start | bytes 294912 | tf_op jit(solution)/shard_map/reduce_scatter | solution.py:284
  1417.6 6.1 copy-start.14
  1418.8 5.1 copy-start.9
  1425.2 324.9 %reduce-scatter.34.cloned.1.call-start = ((), (), s32[]{:S(2)}) async-start(), calls=%async_computation.32 | async-start | bytes 1310720 | tf_op jit(solution)/shard_map/reduce_scatter | solution.py:261
  1459.5 324.0 %reduce-scatter.32.cloned.1.call-start = ((), (), s32[]{:S(2)}) async-start(), calls=%async_computation.31 | async-start | bytes 3145728 | tf_op jit(solution)/shard_map/reduce_scatter | solution.py:56
  1466.2 351.8 %reduce-scatter.24.cloned.1.call-start = ((), (), s32[]{:S(2)}) async-start(), calls=%async_computation.23 | async-start | bytes 3145728 | tf_op jit(solution)/shard_map/reduce_scatter | solution.py:56
  1476.2 406.5 %reduce-scatter.46.cloned.1.call-start = ((), (), s32[]{:S(2)}) async-start(), calls=%async_computation.38 | async-start | bytes 147456
  1572.4 211.1 %copy-start.19 = (f32[1024]{0:T(1024)S(1)}, f32[1024]{0:T(1024)}, u32[]{:S(2)}) copy-start(f32[1024]{0:T(1024)} %copy-done.18) | copy-start | bytes 12292
  1572.4 211.1 %copy-start.22 = (f32[512]{0:T(512)S(1)}, f32[512]{0:T(512)}, u32[]{:S(2)}) copy-start(f32[512]{0:T(512)} %param.21) | copy-start | bytes 6148
  1751.9 66.2 %copy-start.21 = (f32[1024]{0:T(1024)S(1)}, f32[1024]{0:T(1024)}, u32[]{:S(2)}) copy-start(f32[1024]{0:T(1024)} %get-tuple-element.300) | copy-start | bytes 12292
  (56 other events, 116.5 us)
Sparse Core Ops, SparseCore 0:
  21.1 33.3 all-gather.8
  58.4 51.3 all-reduce.3
  112.5 71.7 reduce-scatter.17
  259.0 34.4 all-gather.10
  299.8 31.8 reduce-scatter.19
  333.7 33.1 all-gather.16
  369.1 33.1 all-gather.12
  405.0 166.7 reduce-scatter.25
  574.4 315.9 reduce-scatter.21
  902.2 143.2 all-gather.18
  1064.8 31.8 reduce-scatter.27
  1110.2 32.2 all-gather.20
  1150.1 71.7 reduce-scatter.29
  1223.4 76.1 all-gather.14
  1361.0 56.6 all-reduce.5
  1419.7 33.5 all-gather.22
  1455.5 56.1 reduce-scatter.43
  1514.0 56.0 reduce-scatter.41
  1572.5 56.0 reduce-scatter.39
  1630.8 26.9 reduce-scatter.37
  1661.7 59.8 reduce-scatter.35
  1723.9 26.1 reduce-scatter.33
  1753.0 30.4 reduce-scatter.31
  1786.2 31.8 reduce-scatter.23
  1821.7 60.8 reduce-scatter.45
where the time goes:
time: 1900 us; the launch traced here: 1890 us
  waiting for transfers between devices  1390 us (73%)
  matrix products  303 us (16%)
  other arithmetic  86.5 us (5%)
  local copies, waits for them, and re-layouts  63 us (3%)
  blocking collectives  28.9 us (2%)
    reduce_scatter x4, waiting for transfers between devices, spread_rows(): lax.psum_scatter(lax.dot_general(gathered, matrix, (((1,), (contract_dim,...  587 us
    all_gather x4, waiting for transfers between devices, fold_rows(): shard_rows = lax.all_gather(operand, 'row', axis=0, tiled=True)  206 us
    reduce_scatter x4, waiting for transfers between devices, spread_columns(): lax.psum_scatter(operand.astype(jnp.bfloat16), 'col', scatter_dimension=0...  116 us
    all_gather x4, waiting for transfers between devices, gather_columns(): return lax.all_gather(operand, 'col', axis=0, tiled=True)  105 us
    dot_general x4, matrix products, spread_rows(): lax.dot_general(gathered, matrix, (((1,), (contract_dim,)), ((), ())), pr...  62.7 us
    reduce_scatter x1, waiting for transfers between devices, per_device(): lax.psum_scatter(grad_kv_local.astype(jnp.bfloat16), ('dp', 'col'), scatt...  62 us
    unnamed x26, waiting for transfers between devices  60.7 us
    reduce_scatter x1, waiting for transfers between devices, per_device(): lax.psum_scatter(grad_both_local[:, :ff_local].astype(jnp.bfloat16), 'dp'...  56.2 us
  transfers between devices with their start and end apart: 25, of which 24 were waited for; matrix products, arithmetic and copies ran while one was open for 15% of the time, Pallas kernels for 0%

commit v1 on v0

--- a/solution.py
+++ b/solution.py
@@ -9,6 +9,27 @@
 MASKED = -1e30
 CONTRACT_ROWS = (((0,), (0,)), ((), ()))
 CONTRACT_LAST = (((1,), (1,)), ((), ()))
+
+
+def ring_gather(shard, axis, dim):
+    size, index, rows = (lax.axis_size(axis), lax.axis_index(axis), shard.shape[dim])
+    upward = [(i, (i + 1) % size) for i in range(size)]
+    downward = [(i, (i - 1) % size) for i in range(size)]
+    result = jnp.zeros((*shard.shape[:dim], size * rows, *shard.shape[dim + 1 :]), shard.dtype)
+    result = lax.dynamic_update_slice_in_dim(result, shard, index * rows, axis=dim)
+    from_left = from_right = shard
+    half = size // 2
+    for step in range(1, half + 1):
+        from_left = lax.ppermute(from_left, axis, upward)
+        result = lax.dynamic_update_slice_in_dim(
+            result, from_left, (index - step) % size * rows, axis=dim
+        )
+        if step < size - half:
+            from_right = lax.ppermute(from_right, axis, downward)
+            result = lax.dynamic_update_slice_in_dim(
+                result, from_right, (index + step) % size * rows, axis=dim
+            )
+    return result
 
 
 def rope_tables(positions, head_width):
@@ -77,7 +98,7 @@
     grad_shape = (partner.shape[1], operand.shape[1]) if partner is not None else (1, 1)
     grad_zero = jnp.zeros(grad_shape, jnp.float32)
     kept_zero = jnp.zeros((full_rows, operand.shape[1]) if keeping else (1, 1), operand.dtype)
-    shard_rows = lax.all_gather(operand, "row", axis=0, tiled=True)
+    shard_rows = ring_gather(operand, "row", 0)
     grad_acc = grad_zero
     kept_rows = kept_zero
     row_block = lax.dot_general(

time: 1900 us -> 2030 us (1.068)
  local copies, waits for them, and re-layouts: 63 us -> 120 us
  waiting for transfers between devices: 1390 us -> 1440 us
    ppermute x0 -> x12, waiting for transfers between devices: none -> 359 us  [the longest x8 359 us: ring_gather(): from_left = lax.ppermute(from_left, axis, upward)]
    all_gather x4 -> x0, waiting for transfers between devices: 206 us -> none  [fold_rows(): shard_rows = lax.all_gather(operand, 'row', axis=0, tiled=True)]
    reduce_scatter x4, waiting for transfers between devices: 587 us -> 515 us  [spread_rows(): lax.psum_scatter(lax.dot_general(gathered, matrix, (((1,), (contract_dim,...]
    dynamic_update_slice x0 -> x14, local copies, waits for them, and re-layouts: none -> 33.1 us  [the longest x8 20.5 us: ring_gather(): lax.dynamic_update_slice_in_dim(result, from_left, (index - step) % size...]
    reduce_scatter x1, waiting for transfers between devices: 35.5 us -> 9.72 us  [per_device(): lax.psum_scatter(grad_down_local.astype(jnp.bfloat16), 'dp', scatter_dime...]
    unnamed x26 -> x22, waiting for transfers between devices: 60.7 us -> 59.6 us
  transfers between devices with their start and end apart: 25 -> 33, of which waited for: 24 -> 28; matrix products, arithmetic and copies ran while one was open for 15% -> 11% of each run, Pallas kernels for 0% -> 0%
where the time goes in v1:
time: 2030 us; the launch traced here: 2020 us
  waiting for transfers between devices  1440 us (71%)
  matrix products  299 us (15%)
  local copies, waits for them, and re-layouts  120 us (6%)
  other arithmetic  103 us (5%)
  blocking collectives  28.9 us (1%)
    reduce_scatter x4, waiting for transfers between devices, spread_rows(): lax.psum_scatter(lax.dot_general(gathered, matrix, (((1,), (contract_dim,...  515 us
    ppermute x8, waiting for transfers between devices, ring_gather(): from_left = lax.ppermute(from_left, axis, upward)  359 us
    reduce_scatter x4, waiting for transfers between devices, spread_columns(): lax.psum_scatter(operand.astype(jnp.bfloat16), 'col', scatter_dimension=0...  115 us
    all_gather x4, waiting for transfers between devices, gather_columns(): return lax.all_gather(operand, 'col', axis=0, tiled=True)  105 us
    dot_general x4, matrix products, spread_rows(): lax.dot_general(gathered, matrix, (((1,), (contract_dim,)), ((), ())), pr...  62.7 us
    reduce_scatter x1, waiting for transfers between devices, per_device(): lax.psum_scatter(grad_kv_local.astype(jnp.bfloat16), ('dp', 'col'), scatt...  61.9 us
    unnamed x22, waiting for transfers between devices  59.6 us
    reduce_scatter x1, waiting for transfers between devices, per_device(): lax.psum_scatter(grad_both_local[:, :ff_local].astype(jnp.bfloat16), 'dp'...  56 us
  transfers between devices with their start and end apart: 33, of which 28 were waited for; matrix products, arithmetic and copies ran while one was open for 11% of the time, Pallas kernels for 0%

profile of v1, /device:TPU:0, one launch (start us, length us, event | category | flops | bytes accessed | tf_op | source)
XLA Modules:
  0.0 2020.8 jit_solution(3905626334866049143)
XLA Ops:
  8.9 8.4 psum.49
  21.1 33.5 %all-gather.5.cloned.1.call-done = bf16[2048,512]{1,0:T(8,128)(2,1)} async-done(((bf16[1024,512]{1,0:T(8,128)(2,1)}), bf16[2048,512]{1,0:T(8,128)(2,1)}) %all-gather.5.cloned.1.call-update) | async-done | bytes 2097168 | tf_op jit(solution)/shard_map/all_gather | solution.py:73
  58.3 7.5 fusion.66
  70.2 39.6 %all-reduce.4.cloned.1.call-done = f32[2048,256]{1,0:T(8,128)} async-done(((f32[2048,256]{1,0:T(8,128)}), f32[2048,256]{1,0:T(8,128)}) %all-reduce.4.cloned.1.call-update) | async-done | bytes 2097168 | tf_op jit(solution)/shard_map/psum | solution.py:160
  109.8 7.8 fusion.54
  122.4 62.0 %reduce-scatter.18.cloned.1.call-done = f32[512,1024]{1,0:T(8,128)} async-done(((f32[2048,1024]{1,0:T(8,128)}), f32[512,1024]{1,0:T(8,128)}) %reduce-scatter.18.cloned.1.call-update) | async-done | bytes 2097168 | tf_op jit(solution)/shard_map/reduce_scatter | solution.py:83
  192.5 72.4 %while.30 = (s32[]{:T(128)}, bf16[8,512,128]{1,2,0:T(8,128)(2,1)}, f32[8,512]{1,0:T(8,128)S(1)}, bf16[8,512,128]{2,1,0:T(8,128)(2,1)}, bf16[2048,128]{1,0:T(8,12...) while((s32[]{:T(128)}, bf16[8,512,128]{1,2,0:T(8,128)(2,1)}, ...), condition=%wide.region_7.8_spmd.clone.clone, body=%wide.region_4.7_spmd.clone.sunk.clone | while | flops 548404736 | bytes 30844036 | solution.py:190
  266.6 23.5 %collective-permute-done = bf16[512,1024]{0,1:T(8,128)(2,1)} collective-permute-done((bf16[512,1024]{0,1:T(8,128)(2,1)}, bf16[512,1024]{0,1:T(8,128)(2,1)}, u32[]{:S(2)}, u32[]{:S(2)}) %collective-permute-start) | collective-permute-done | bytes 1048608 | tf_op jit(solution)/shard_map/ppermute | solution.py:23
  294.6 10.2 collective-permute-done.2
  314.8 28.9 %reduce-scatter.20.cloned.1.call-done = bf16[1024,512]{1,0:T(8,128)(2,1)} async-done(((bf16[2048,512]{1,0:T(8,128)(2,1)}), bf16[1024,512]{1,0:T(8,128)(2,1)}) %reduce-scatter.20.cloned.1.call-update) | async-done | bytes 1048592 | tf_op jit(solution)/shard_map/reduce_scatter | solution.py:77
  345.7 6.9 psum.51
  355.8 23.1 %all-gather.9.cloned.1.call-done = bf16[2048,512]{1,0:T(8,128)(2,1)} async-done(((bf16[1024,512]{1,0:T(8,128)(2,1)}), bf16[2048,512]{1,0:T(8,128)(2,1)}) %all-gather.9.cloned.1.call-update) | async-done | bytes 2097168 | tf_op jit(solution)/shard_map/all_gather | solution.py:73
  378.9 13.4 fusion.69
  398.0 16.1 all-gather.7.cloned.1.call-done
  414.1 34.3 %fusion.68 = f32[2048,5632]{1,0:T(8,128)} fusion(bf16[2048,512]{1,0:T(8,128)(2,1)} %all-gather.7.cloned.1.call-done, bf16[512,5632]{1,0:T(8,128)(2,1)} %constant_dynamic-update-slice_fusion.1), kind=kOutput, calls=%fused_computation.154 | convolution fusion | flops 11811160064 | bytes 54001664 | tf_op jit(solution)/shard_map/dot_general | solution.py:84
  448.9 134.9 %reduce-scatter.26.cloned.1.call-done = f32[512,2816]{1,0:T(8,128)} async-done(((f32[2048,2816]{1,0:T(8,128)}), f32[512,2816]{1,0:T(8,128)}) %reduce-scatter.26.cloned.1.call-update) | async-done | bytes 5767184 | tf_op jit(solution)/shard_map/reduce_scatter | solution.py:83
  583.7 318.6 %reduce-scatter.22.cloned.1.call-done = f32[512,5632]{1,0:T(8,128)} async-done(((f32[2048,5632]{1,0:T(8,128)}), f32[512,5632]{1,0:T(8,128)}) %reduce-scatter.22.cloned.1.call-update) | async-done | bytes 11534352 | tf_op jit(solution)/shard_map/reduce_scatter | solution.py:83
  902.3 9.0 multiply_convert_fusion.2
  911.3 8.0 broadcast_in_dim.86
  919.3 7.7 pad_maximum_fusion
  928.7 124.4 %collective-permute-done.6 = bf16[512,5632]{1,0:T(8,128)(2,1)S(1)} collective-permute-done((bf16[512,5632]{1,0:T(8,128)(2,1)}, bf16[512,5632]{1,0:T(8,128)(2,1)S(1)}, u32[]{:S(2)}, u32[]{:S(2)}) %collective-permute-start.6) | collective-permute-done | bytes 5767200 | tf_op jit(solution)/shard_map/ppermute | solution.py:23
  1058.9 59.0 %collective-permute-done.8 = bf16[512,5632]{1,0:T(8,128)(2,1)S(1)} collective-permute-done((bf16[512,5632]{1,0:T(8,128)(2,1)S(1)}, bf16[512,5632]{1,0:T(8,128)(2,1)S(1)}, u32[]{:S(2)}, u32[]{:S(2)}) %collective-permute-start.8) | collective-permute-done | bytes 5767200 | tf_op jit(solution)/shard_map/ppermute | solution.py:23
  1120.7 19.2 convolution_convert_fusion.2
  1139.9 31.7 %reduce-scatter.28.cloned.1.call-done = bf16[1024,512]{1,0:T(8,128)(2,1)} async-done(((bf16[2048,512]{1,0:T(8,128)(2,1)}), bf16[1024,512]{1,0:T(8,128)(2,1)}) %reduce-scatter.28.cloned.1.call-update) | async-done | bytes 1048592 | tf_op jit(solution)/shard_map/reduce_scatter | solution.py:77
  1175.0 6.8 psum.52
  1185.7 32.3 %all-gather.11.cloned.1.call-done = bf16[2048,512]{1,0:T(8,128)(2,1)} async-done(((bf16[1024,512]{1,0:T(8,128)(2,1)}), bf16[2048,512]{1,0:T(8,128)(2,1)}) %all-gather.11.cloned.1.call-update) | async-done | bytes 2097168 | tf_op jit(solution)/shard_map/all_gather | solution.py:73
  1218.0 7.5 fusion.70
  1230.7 9.7 constant_dynamic-update-slice_fusion.14
  1242.1 106.4 %collective-permute-done.3 = bf16[512,2816]{1,0:T(8,128)(2,1)} collective-permute-done((bf16[512,2816]{1,0:T(8,128)(2,1)}, bf16[512,2816]{1,0:T(8,128)(2,1)}, u32[]{:S(2)}, u32[]{:S(2)}) %collective-permute-start.3) | collective-permute-done | bytes 2883616 | tf_op jit(solution)/shard_map/ppermute | solution.py:23
  1356.0 26.7 %collective-permute-done.5 = bf16[512,2816]{1,0:T(8,128)(2,1)} collective-permute-done((bf16[512,2816]{1,0:T(8,128)(2,1)}, bf16[512,2816]{1,0:T(8,128)(2,1)}, u32[]{:S(2)}, u32[]{:S(2)}) %collective-permute-start.5) | collective-permute-done | bytes 2883616 | tf_op jit(solution)/shard_map/ppermute | solution.py:23
  1389.0 131.3 %while.31 = (s32[]{:T(128)}, f32[2048,128]{1,0:T(8,128)}, f32[2048,128]{1,0:T(8,128)}, f32[8,512,128]{1,2,0:T(8,128)}, bf16[8,512,128]{2,1,0:T(8,128)(2,1)}, /*i...) while((s32[]{:T(128)}, f32[2048,128]{1,0:T(8,128)}, ...), condition=%wide.region_20.21_spmd.clone.clone, body=%wide.region_18.20_spmd.clone.sunk.clone | while | flops 1356135936 | bytes 87327544 | solution.py:256
  1524.6 10.8 convolution_convert_fusion.1
  1535.7 17.5 convolution_convert_fusion
  1556.7 6.3 convolution_convert_fusion.6
  1572.7 10.3 all-reduce.6.cloned.1.call-done
  1584.2 8.9 collective-permute-done.9
  1615.7 6.2 convolution_convert_fusion.3
  1622.0 10.0 convolution_convert_fusion.5
  1632.0 9.7 reduce-scatter.44.cloned.1.call-done
  1644.2 55.9 %reduce-scatter.42.cloned.1.call-done = bf16[128,2816]{1,0:T(8,128)(2,1)} async-done(((bf16[512,2816]{1,0:T(8,128)(2,1)}), bf16[128,2816]{1,0:T(8,128)(2,1)}) %reduce-scatter.42.cloned.1.call-update) | async-done | bytes 720912 | tf_op jit(solution)/shard_map/reduce_scatter | solution.py:294
  1702.4 56.0 %reduce-scatter.40.cloned.1.call-done = bf16[128,2816]{1,0:T(8,128)(2,1)} async-done(((bf16[512,2816]{1,0:T(8,128)(2,1)}), bf16[128,2816]{1,0:T(8,128)(2,1)}) %reduce-scatter.40.cloned.1.call-update) | async-done | bytes 720912 | tf_op jit(solution)/shard_map/reduce_scatter | solution.py:288
  1760.7 27.0 %reduce-scatter.38.cloned.1.call-done = bf16[256,512]{1,0:T(8,128)(2,1)} async-done(((bf16[1024,512]{1,0:T(8,128)(2,1)}), bf16[256,512]{1,0:T(8,128)(2,1)}) %reduce-scatter.38.cloned.1.call-update) | async-done | bytes 262160 | tf_op jit(solution)/shard_map/reduce_scatter | solution.py:285
  1789.5 61.9 %reduce-scatter.36.cloned.1.call-done = bf16[64,256]{1,0:T(8,128)(2,1)} async-done(((bf16[512,256]{1,0:T(8,128)(2,1)}), bf16[64,256]{1,0:T(8,128)(2,1)}) %reduce-scatter.36.cloned.1.call-update) | async-done | bytes 32784 | tf_op jit(solution)/shard_map/reduce_scatter | solution.py:305
  1852.7 27.0 %reduce-scatter.34.cloned.1.call-done = bf16[128,1024]{1,0:T(8,128)(2,1)} async-done(((bf16[512,1024]{1,0:T(8,128)(2,1)}), bf16[128,1024]{1,0:T(8,128)(2,1)}) %reduce-scatter.34.cloned.1.call-update) | async-done | bytes 262160 | tf_op jit(solution)/shard_map/reduce_scatter | solution.py:282
  1881.5 31.6 %reduce-scatter.32.cloned.1.call-done = bf16[1024,512]{1,0:T(8,128)(2,1)} async-done(((bf16[2048,512]{1,0:T(8,128)(2,1)}), bf16[1024,512]{1,0:T(8,128)(2,1)}) %reduce-scatter.32.cloned.1.call-update) | async-done | bytes 1048592 | tf_op jit(solution)/shard_map/reduce_scatter | solution.py:77
  1917.7 6.9 psum.55
  1924.6 23.0 %reduce-scatter.24.cloned.1.call-done = bf16[1024,512]{1,0:T(8,128)(2,1)} async-done(((bf16[2048,512]{1,0:T(8,128)(2,1)}), bf16[1024,512]{1,0:T(8,128)(2,1)}) %reduce-scatter.24.cloned.1.call-update) | async-done | bytes 1048592 | tf_op jit(solution)/shard_map/reduce_scatter | solution.py:77
  1953.5 58.7 %reduce-scatter.46.cloned.1.call-done = bf16[64,2]{1,0:T(8,128)(2,1)} async-done(((bf16[512,2]{1,0:T(8,128)(2,1)}), bf16[64,2]{1,0:T(8,128)(2,1)}) %reduce-scatter.46.cloned.1.call-update) | async-done | bytes 272
  (426 shorter events, 360.1 us)
Async XLA Ops:
  7.2 371.7 %copy-start = (bf16[2816,512]{1,0:T(8,128)(2,1)S(1)}, bf16[2816,512]{1,0:T(8,128)(2,1)}, u32[]{:S(2)}) copy-start(bf16[2816,512]{1,0:T(8,128)(2,1)} %param.28) | copy-start | bytes 8650756
  7.2 47.4 %copy-start.17 = (bf16[512,256]{1,0:T(8,128)(2,1)S(1)}, bf16[512,256]{1,0:T(8,128)(2,1)}, u32[]{:S(2)}) copy-start(bf16[512,256]{1,0:T(8,128)(2,1)} %param.24) | copy-start | bytes 786436
  7.2 47.4 %all-gather.5.cloned.1.call-start = ((), (), s32[]{:S(2)}) async-start(), calls=%async_computation.15 | async-start | bytes 3145728 | tf_op jit(solution)/shard_map/all_gather | solution.py:73
  21.0 88.7 %all-reduce.4.cloned.1.call-start = ((), (), s32[]{:S(2)}) async-start(), calls=%async_computation.17 | async-start | bytes 4194304 | tf_op jit(solution)/shard_map/psum | solution.py:160
  58.2 126.1 %reduce-scatter.18.cloned.1.call-start = ((), (), s32[]{:S(2)}) async-start(), calls=%async_computation.16 | async-start | bytes 10485760 | tf_op jit(solution)/shard_map/reduce_scatter | solution.py:83
  65.8 277.9 %reduce-scatter.20.cloned.1.call-start = ((), (), s32[]{:S(2)}) async-start(), calls=%async_computation.18 | async-start | bytes 3145728 | tf_op jit(solution)/shard_map/reduce_scatter | solution.py:77
  66.5 51.1 %copy-start.20 = (f32[2048]{0:T(1024)}, f32[2048]{0:T(1024)S(1)}, u32[]{:S(2)}) copy-start(f32[2048]{0:T(1024)S(1)} %convert_element_type.116) | copy-start | bytes 24580
  69.1 48.4 %copy-start.36 = (f32[64]{0:T(128)}, f32[64]{0:T(128)S(1)}, u32[]{:S(2)}) copy-start(f32[64]{0:T(128)S(1)} %multiply_power_fusion) | copy-start | bytes 772
  117.7 69.5 %copy-start.13 = (f32[512,64]{0,1:T(8,128)}, f32[512,64]{0,1:T(8,128)S(1)}, u32[]{:S(2)}) copy-start(f32[512,64]{0,1:T(8,128)S(1)} %copy.36) | copy-start | bytes 393220
  264.9 25.2 %collective-permute-start = (bf16[512,1024]{0,1:T(8,128)(2,1)}, bf16[512,1024]{0,1:T(8,128)(2,1)}, u32[]{:S(2)}, u32[]{:S(2)}) collective-permute-start(bf16[512,1024]{0,1:T(8,128)(2,1)} %bitcast.150), channel_id=1, source_target_pairs={{0,2},{2,4},{4,6},{6,0},{1,3},{3,5},{5,7},{7,1},{8,10},{10,12},{12... | collective-permute-start | bytes 3145736 | tf_op jit(solution)/shard_map/ppermute | solution.py:23
  264.9 28.4 %collective-permute-start.1 = (bf16[512,1024]{0,1:T(8,128)(2,1)}, bf16[512,1024]{0,1:T(8,128)(2,1)}, u32[]{:S(2)}, u32[]{:S(2)}) collective-permute-start(bf16[512,1024]{0,1:T(8,128)(2,1)} %bitcast.151), channel_id=1, source_target_pairs={{0,6},{2,0},{4,2},{6,4},{1,7},{3,1},{5,3},{7,5},{8,14},{10,8},{12,... | collective-permute-start | bytes 3145736 | tf_op jit(solution)/shard_map/ppermute | solution.py:28
  290.1 14.7 collective-permute-start.2
  312.0 40.6 %copy-start.28 = (f32[512]{0:T(512)S(1)}, f32[512]{0:T(512)}, u32[]{:S(2)}) copy-start(f32[512]{0:T(512)} %param.22) | copy-start | bytes 6148
  312.0 66.9 %all-gather.9.cloned.1.call-start = ((), (), s32[]{:S(2)}) async-start(), calls=%async_computation.22 | async-start | bytes 3145728 | tf_op jit(solution)/shard_map/all_gather | solution.py:73
  314.8 99.3 %all-gather.7.cloned.1.call-start = ((), (), s32[]{:S(2)}) async-start(), calls=%async_computation.19 | async-start | bytes 3145728 | tf_op jit(solution)/shard_map/all_gather | solution.py:73
  352.6 829.2 %copy-start.18 = (f32[1024]{0:T(1024)}, f32[1024]{0:T(1024)S(1)}, u32[]{:S(2)}) copy-start(f32[1024]{0:T(1024)S(1)} %get-tuple-element.306) | copy-start | bytes 12292
  352.6 829.2 %copy-start.24 = (f32[1024]{0:T(1024)}, f32[1024]{0:T(1024)S(1)}, u32[]{:S(2)}) copy-start(f32[1024]{0:T(1024)S(1)} %get-tuple-element.305) | copy-start | bytes 12292
  355.7 228.0 %reduce-scatter.26.cloned.1.call-start = ((), (), s32[]{:S(2)}) async-start(), calls=%async_computation.23 | async-start | bytes 28835840 | tf_op jit(solution)/shard_map/reduce_scatter | solution.py:83
  392.4 509.9 %reduce-scatter.22.cloned.1.call-start = ((), (), s32[]{:S(2)}) async-start(), calls=%async_computation.20 | async-start | bytes 57671680 | tf_op jit(solution)/shard_map/reduce_scatter | solution.py:83
  448.4 723.2 %reduce-scatter.28.cloned.1.call-start = ((), (), s32[]{:S(2)}) async-start(), calls=%async_computation.24 | async-start | bytes 3145728 | tf_op jit(solution)/shard_map/reduce_scatter | solution.py:77
  927.0 126.1 %collective-permute-start.6 = (bf16[512,5632]{1,0:T(8,128)(2,1)}, bf16[512,5632]{1,0:T(8,128)(2,1)S(1)}, u32[]{:S(2)}, u32[]{:S(2)}) collective-permute-start(bf16[512,5632]{1,0:T(8,128)(2,1)} %get-tuple-element.289), channel_id=1, source_target_pairs={{0,2},{2,4},{4,6},{6,0},{1,3},{3,5},{5,7},{7,1},{8,10},{10,12},{12... | collective-permute-start | bytes 17301512 | tf_op jit(solution)/shard_map/ppermute | solution.py:23
  927.0 129.0 %collective-permute-start.7 = (bf16[512,5632]{1,0:T(8,128)(2,1)}, bf16[512,5632]{1,0:T(8,128)(2,1)S(1)}, u32[]{:S(2)}, u32[]{:S(2)}) collective-permute-start(bf16[512,5632]{1,0:T(8,128)(2,1)} %get-tuple-element.289), channel_id=1, source_target_pairs={{0,6},{2,0},{4,2},{6,4},{1,7},{3,1},{5,3},{7,5},{8,14},{10,8},{12,... | collective-permute-start | bytes 17301512 | tf_op jit(solution)/shard_map/ppermute | solution.py:28
  1053.1 64.8 %collective-permute-start.8 = (bf16[512,5632]{1,0:T(8,128)(2,1)S(1)}, bf16[512,5632]{1,0:T(8,128)(2,1)S(1)}, u32[]{:S(2)}, u32[]{:S(2)}) collective-permute-start(bf16[512,5632]{1,0:T(8,128)(2,1)S(1)} %collective-permute-done.6), channel_id=1, source_target_pairs={{0,2},{2,4},{4,6},{6,0},{1,3},{3,5},{5,7},{7,1},{8,10},{10,12},{12... | collective-permute-start | bytes 17301512 | tf_op jit(solution)/shard_map/ppermute | solution.py:23
  1139.9 78.1 %all-gather.11.cloned.1.call-start = ((), (), s32[]{:S(2)}) async-start(), calls=%async_computation.25 | async-start | bytes 3145728 | tf_op jit(solution)/shard_map/all_gather | solution.py:73
  1185.6 200.7 %reduce-scatter.30.cloned.1.call-start = ((), (), s32[]{:S(2)}) async-start(), calls=%async_computation.26 | async-start | bytes 10485760 | tf_op jit(solution)/shard_map/reduce_scatter | solution.py:83
  1225.6 357.4 %all-reduce.6.cloned.1.call-start = ((), (), s32[]{:S(2)}) async-start(), calls=%async_computation.35 | async-start | bytes 2097152 | tf_op jit(solution)/shard_map/psum | solution.py:260
  1240.4 108.1 %collective-permute-start.3 = (bf16[512,2816]{1,0:T(8,128)(2,1)}, bf16[512,2816]{1,0:T(8,128)(2,1)}, u32[]{:S(2)}, u32[]{:S(2)}) collective-permute-start(bf16[512,2816]{1,0:T(8,128)(2,1)} %get-tuple-element.280), channel_id=1, source_target_pairs={{0,2},{2,4},{4,6},{6,0},{1,3},{3,5},{5,7},{7,1},{8,10},{10,12},{12... | collective-permute-start | bytes 8650760 | tf_op jit(solution)/shard_map/ppermute | solution.py:23
  1240.4 112.0 %collective-permute-start.4 = (bf16[512,2816]{1,0:T(8,128)(2,1)}, bf16[512,2816]{1,0:T(8,128)(2,1)}, u32[]{:S(2)}, u32[]{:S(2)}) collective-permute-start(bf16[512,2816]{1,0:T(8,128)(2,1)} %get-tuple-element.280), channel_id=1, source_target_pairs={{0,6},{2,0},{4,2},{6,4},{1,7},{3,1},{5,3},{7,5},{8,14},{10,8},{12,... | collective-permute-start | bytes 8650760 | tf_op jit(solution)/shard_map/ppermute | solution.py:28
  1348.5 34.2 %collective-permute-start.5 = (bf16[512,2816]{1,0:T(8,128)(2,1)}, bf16[512,2816]{1,0:T(8,128)(2,1)}, u32[]{:S(2)}, u32[]{:S(2)}) collective-permute-start(bf16[512,2816]{1,0:T(8,128)(2,1)} %collective-permute-done.3), channel_id=1, source_target_pairs={{0,2},{2,4},{4,6},{6,0},{1,3},{3,5},{5,7},{7,1},{8,10},{10,12},{12... | collective-permute-start | bytes 8650760 | tf_op jit(solution)/shard_map/ppermute | solution.py:23
  1524.5 117.2 %reduce-scatter.44.cloned.1.call-start = ((), (), s32[]{:S(2)}) async-start(), calls=%async_computation.33 | async-start | bytes 3604480 | tf_op jit(solution)/shard_map/reduce_scatter | solution.py:300
  1535.4 164.6 %reduce-scatter.42.cloned.1.call-start = ((), (), s32[]{:S(2)}) async-start(), calls=%async_computation.32 | async-start | bytes 3604480 | tf_op jit(solution)/shard_map/reduce_scatter | solution.py:294
  1556.1 202.3 %reduce-scatter.40.cloned.1.call-start = ((), (), s32[]{:S(2)}) async-start(), calls=%async_computation.31 | async-start | bytes 3604480 | tf_op jit(solution)/shard_map/reduce_scatter | solution.py:288
  1556.7 231.0 %reduce-scatter.38.cloned.1.call-start = ((), (), s32[]{:S(2)}) async-start(), calls=%async_computation.30 | async-start | bytes 1310720 | tf_op jit(solution)/shard_map/reduce_scatter | solution.py:285
  1563.1 288.2 %reduce-scatter.36.cloned.1.call-start = ((), (), s32[]{:S(2)}) async-start(), calls=%async_computation.29 | async-start | bytes 294912 | tf_op jit(solution)/shard_map/reduce_scatter | solution.py:305
  1566.1 27.0 %collective-permute-start.9 = (bf16[512,1024]{0,1:T(8,128)(2,1)}, bf16[512,1024]{0,1:T(8,128)(2,1)}, u32[]{:S(2)}, u32[]{:S(2)}) collective-permute-start(bf16[512,1024]{0,1:T(8,128)(2,1)} %bitcast.6), channel_id=1, source_target_pairs={{0,2},{2,4},{4,6},{6,0},{1,3},{3,5},{5,7},{7,1},{8,10},{10,12},{12... | collective-permute-start | bytes 3145736 | tf_op jit(solution)/shard_map/ppermute | solution.py:23
  1566.4 38.9 %collective-permute-start.10 = (bf16[512,1024]{0,1:T(8,128)(2,1)}, bf16[512,1024]{0,1:T(8,128)(2,1)}, u32[]{:S(2)}, u32[]{:S(2)}) collective-permute-start(bf16[512,1024]{0,1:T(8,128)(2,1)} %bitcast.6), channel_id=1, source_target_pairs={{0,6},{2,0},{4,2},{6,4},{1,7},{3,1},{5,3},{7,5},{8,14},{10,8},{12,... | collective-permute-start | bytes 3145736 | tf_op jit(solution)/shard_map/ppermute | solution.py:28
  1593.1 14.5 collective-permute-start.11
  1602.5 277.2 %reduce-scatter.34.cloned.1.call-start = ((), (), s32[]{:S(2)}) async-start(), calls=%async_computation.28 | async-start | bytes 1310720 | tf_op jit(solution)/shard_map/reduce_scatter | solution.py:282
  1615.7 297.5 %reduce-scatter.32.cloned.1.call-start = ((), (), s32[]{:S(2)}) async-start(), calls=%async_computation.27 | async-start | bytes 3145728 | tf_op jit(solution)/shard_map/reduce_scatter | solution.py:77
  1621.9 325.7 %reduce-scatter.24.cloned.1.call-start = ((), (), s32[]{:S(2)}) async-start(), calls=%async_computation.21 | async-start | bytes 3145728 | tf_op jit(solution)/shard_map/reduce_scatter | solution.py:77
  1632.0 380.2 %reduce-scatter.46.cloned.1.call-start = ((), (), s32[]{:S(2)}) async-start(), calls=%async_computation.34 | async-start | bytes 147456
  1644.2 269.0 %copy-start.23 = (f32[1024]{0:T(1024)S(1)}, f32[1024]{0:T(1024)}, u32[]{:S(2)}) copy-start(f32[1024]{0:T(1024)} %copy-done.22) | copy-start | bytes 12292
  1644.2 269.0 %copy-start.32 = (f32[512]{0:T(512)S(1)}, f32[512]{0:T(512)}, u32[]{:S(2)}) copy-start(f32[512]{0:T(512)} %param.21) | copy-start | bytes 6148
  1881.5 66.1 %copy-start.19 = (f32[1024]{0:T(1024)S(1)}, f32[1024]{0:T(1024)}, u32[]{:S(2)}) copy-start(f32[1024]{0:T(1024)} %copy-done.18) | copy-start | bytes 12292
  1881.5 66.1 %copy-start.25 = (f32[1024]{0:T(1024)S(1)}, f32[1024]{0:T(1024)}, u32[]{:S(2)}) copy-start(f32[1024]{0:T(1024)} %copy-done.24) | copy-start | bytes 12292
  1881.5 66.1 %copy-start.27 = (f32[1024]{0:T(1024)S(1)}, f32[1024]{0:T(1024)}, u32[]{:S(2)}) copy-start(f32[1024]{0:T(1024)} %copy-done.26) | copy-start | bytes 12292
  1881.5 66.1 %copy-start.29 = (f32[512]{0:T(512)S(1)}, f32[512]{0:T(512)}, u32[]{:S(2)}) copy-start(f32[512]{0:T(512)} %param.22) | copy-start | bytes 6148
  1881.5 66.1 %copy-start.30 = (f32[1024]{0:T(1024)S(1)}, f32[1024]{0:T(1024)}, u32[]{:S(2)}) copy-start(f32[1024]{0:T(1024)} %get-tuple-element.303) | copy-start | bytes 12292
  (75 other events, 310.4 us)
Sparse Core Ops, SparseCore 0:
  21.1 33.3 all-gather.4
  58.3 51.3 all-reduce.3
  112.5 71.7 reduce-scatter.17
  312.1 31.5 reduce-scatter.19
  345.8 33.1 all-gather.8
  381.0 33.1 all-gather.6
  416.9 166.7 reduce-scatter.25
  586.3 315.9 reduce-scatter.21
  1140.0 31.5 reduce-scatter.27
  1185.7 32.2 all-gather.10
  1225.7 119.0 reduce-scatter.29
  1524.6 58.2 all-reduce.5
  1585.4 56.3 reduce-scatter.43
  1644.0 56.0 reduce-scatter.41
  1702.3 56.0 reduce-scatter.39
  1760.7 26.9 reduce-scatter.37
  1791.4 59.8 reduce-scatter.35
  1853.5 26.1 reduce-scatter.33
  1882.6 30.4 reduce-scatter.31
  1915.8 31.8 reduce-scatter.23
  1951.3 60.8 reduce-scatter.45
